TPU v7x, 256 devices: a whole 4x4x8 slice. The times are simulated.
256 devices in a mesh: seq: 16 (over z, core), ch: 16 (over y, x).
Axes of the slice: x: 4, y: 4, z: 8, core: 2. Of those that a mesh axis runs over, the one named last changes fastest.
Arguments:
- query: bfloat16 [2048, 8192], P('seq', 'ch'), may hold values from -6 to 6
- key: bfloat16 [2048, 8192], P('seq', 'ch'), may hold values from -6 to 6
- value: bfloat16 [2048, 8192], P('seq', 'ch'), may hold values from -6 to 6
- short_taps: float32 [3, 3, 8192], P(None, None, 'ch'), may hold values from -3 to 3
- decay_rate: float32 [16, 8192], P(None, 'ch'), may hold values from 0.00012207031 to 0.05
- residue: float32 [16, 8192], P(None, 'ch'), may hold values from -2 to 2
- skip_gain: float32 [8192], P('ch'), may hold values from -4 to 4
- out_weight: bfloat16 [8192, 8192], P('ch', 'seq'), may hold values from -0.09375 to 0.09375
- grad_out: bfloat16 [2048, 8192], P('seq', 'ch'), may hold values from -6 to 6
Outputs:
- mixed: bfloat16 [2048, 8192], P('seq', 'ch')
- grad_query: bfloat16 [2048, 8192], P('seq', 'ch')
- grad_key: bfloat16 [2048, 8192], P('seq', 'ch')
- grad_value: bfloat16 [2048, 8192], P('seq', 'ch')
All inputs are finite; a program needn't handle non-finite values.
Results may differ from a plain program's by a relative error of at most 0.017.
Values may be sent and summed in bfloat16 or wider, within the bound.
A program may use at most 128 MiB of HBM per device.

v0:
```python
import math
import jax
import jax.numpy as jnp
from jax import lax
from jax.sharding import PartitionSpec as P


def from_behind(block, axis, distance):
    devices = range(lax.axis_size(axis))
    route = [(i - distance, i) for i in devices if i - distance in devices]
    return lax.ppermute(block, axis, route)


def entering(shard, axis, join, neutral, backward):
    count = lax.axis_size(axis)
    place = lax.axis_index(axis)
    ahead = count - 1 - place if backward else place
    gathered = jax.tree.map(
        lambda a, kind: lax.all_gather(a.astype(kind), axis), shard, (jnp.bfloat16, jnp.bfloat16)
    )
    state = jax.tree.map(lambda a, e: jnp.zeros_like(a) + jnp.asarray(e, a.dtype), shard, neutral)

    def one(turn, state):
        source = count - 1 - turn if backward else turn
        return join(
            state,
            jax.tree.map(
                lambda a, own: lax.dynamic_index_in_dim(a, source, 0, False).astype(own.dtype),
                gathered,
                shard,
            ),
        )

    return lax.fori_loop(0, ahead, one, state)


def chain_combine(earlier, later):
    return (earlier[0] * later[0], earlier[1] * later[0] + later[1])


def per_device(query, key, value, short_taps, decay_rate, residue, skip_gain, out_weight, grad_out):
    tok_rows, chan_width = query.shape
    tap_count = short_taps.shape[0]
    mode_count = decay_rate.shape[0]
    highest = lax.Precision.HIGHEST
    streams = jnp.stack([query, key, value])
    before = from_behind(streams[:, tok_rows - (tap_count - 1) :, :], "seq", 1)
    extended = jnp.concatenate([before, streams], axis=1).astype(jnp.float32)
    featured = jnp.zeros((3, tok_rows, chan_width), jnp.float32)
    for tap_index in range(tap_count):
        begin = tap_count - 1 - tap_index
        featured = (
            featured + short_taps[tap_index][:, None, :] * extended[:, begin : begin + tok_rows, :]
        )
    q_short = featured[0]
    k_short = featured[1]
    v_short = featured[2]
    gated = k_short * v_short
    columns = lax.all_gather(out_weight, "seq", axis=1, tiled=True)
    block_len = math.gcd(tok_rows, 128)
    block_count = tok_rows // block_len
    mode_scale = residue * jnp.sqrt(-jnp.expm1(-2.0 * decay_rate))
    offsets = jnp.arange(block_len).astype(jnp.float32)
    decay_pos = jnp.exp(-decay_rate[None, :, :] * offsets[:, None, None])
    filter_block = jnp.sum(mode_scale[None, :, :] * decay_pos, axis=1)
    filter_padded = jnp.concatenate(
        [jnp.zeros((block_len, chan_width), jnp.float32), filter_block], axis=0
    )
    lag_steps = jnp.arange(block_len)
    lag_index = block_len + lag_steps[:, None] - lag_steps[None, :]
    toeplitz = jnp.take(filter_padded, lag_index, axis=0)
    to_end = jnp.flip(decay_pos, 0)
    from_entry = mode_scale[None, :, :] * decay_pos * jnp.exp(-decay_rate)[None, :, :]
    step_decay = jnp.exp(-decay_rate * block_len)
    device_decay = jnp.exp(-decay_rate * tok_rows)
    block_steps = jnp.arange(block_count).astype(jnp.float32)
    block_decay = jnp.exp(-decay_rate[None, :, :] * block_len * block_steps[:, None, None])

    def local_pass(signal):
        blocks = signal.reshape(block_count, block_len, chan_width)
        intra = jnp.einsum("ijc,bjc->bic", toeplitz, blocks, precision=highest)
        ends = jnp.einsum("jnc,bjc->bnc", to_end, blocks, precision=highest)

        def advance(state, end_state):
            return (state * step_decay + end_state, state)

        final, entries = lax.scan(advance, jnp.zeros((mode_count, chan_width), jnp.float32), ends)
        return (intra, entries, final)

    def finish(intra, entries, entry_dev):
        starts = entries + block_decay * entry_dev[None, :, :]
        result = intra + jnp.einsum("inc,bnc->bic", from_entry, starts, precision=highest)
        return result.reshape(tok_rows, chan_width)

    def carried(final, later):
        identity = (jnp.ones_like(device_decay), jnp.zeros_like(final))
        if later:
            prefix = entering((device_decay, final), "seq", chain_combine, identity, True)
        else:
            prefix = entering((device_decay, final), "seq", chain_combine, identity, False)
        return prefix[1]

    intra, entries, final = local_pass(gated)
    entry_dev = carried(final, False)
    long_out = finish(intra, entries, entry_dev) + skip_gain[None, :] * gated
    mixer = (q_short * long_out).astype(jnp.bfloat16)
    partial_value = jnp.dot(mixer, columns, preferred_element_type=jnp.float32)
    mixed = lax.psum_scatter(
        partial_value.astype(jnp.bfloat16), "ch", scatter_dimension=1, tiled=True
    )
    grad_mixer = lax.dot_general(
        lax.all_gather(grad_out, "ch", axis=1, tiled=True),
        columns,
        (((1,), (1,)), ((), ())),
        preferred_element_type=jnp.float32,
    )
    grad_qshort = grad_mixer * long_out
    grad_long = grad_mixer * q_short
    intra_b, entries_b, final_b = local_pass(jnp.flip(grad_long, 0))
    exit_dev = carried(final_b, True)
    grad_gated = jnp.flip(finish(intra_b, entries_b, exit_dev), 0) + skip_gain[None, :] * grad_long
    grad_stack = jnp.stack([grad_qshort, grad_gated * v_short, grad_gated * k_short])
    after = from_behind(grad_stack[:, : tap_count - 1, :], "seq", -1)
    extended_back = jnp.concatenate([grad_stack, after], axis=1)
    grads = jnp.zeros((3, tok_rows, chan_width), jnp.float32)
    for tap_index in range(tap_count):
        grads = (
            grads
            + short_taps[tap_index][:, None, :]
            * extended_back[:, tap_index : tap_index + tok_rows, :]
        )
    grads = grads.astype(jnp.bfloat16)
    return (mixed, grads[0], grads[1], grads[2])


def solution(mesh):
    in_specs = (
        P("seq", "ch"),
        P("seq", "ch"),
        P("seq", "ch"),
        P(None, None, "ch"),
        P(None, "ch"),
        P(None, "ch"),
        P("ch"),
        P("ch", "seq"),
        P("seq", "ch"),
    )
    out_specs = (P("seq", "ch"), P("seq", "ch"), P("seq", "ch"), P("seq", "ch"))
    return jax.shard_map(
        per_device, mesh=mesh, in_specs=in_specs, out_specs=out_specs, check_vma=False
    )
```

profile of v0, /device:TPU:32, one launch (start us, length us, event | category | flops | bytes accessed | tf_op | source)
XLA Modules:
  0.0 294.9 jit_solution(6199740509660682278)
XLA Ops:
  7.2 0.7 all-gather.8.cloned.1.call-update
  7.9 0.7 all-gather.6.cloned.1.call-update
  8.7 0.7 pad_maximum_fusion.2
  9.4 1.9 collective-permute-start
  11.4 0.7 slice_bitcast_fusion.6
  12.1 0.8 sqrt_multiply_fusion
  12.9 3.1 %multiply_exponential_fusion = (f32[128,16,512]{2,1,0:T(8,128)}, f32[128,512]{1,0:T(8,128)S(1)}) fusion(f32[128]{0:T(128)S(1)} %iota_convert_fusion, f32[16,512]{1,0:T(8,128)S(1)} %get-tuple-element.208, f32[16,512]{1,0:T(8,128)S(1)} %get-tuple-element.207), kind=kLoop, calls=%fused_computation.12 | loop fusion | flops 3080192 | bytes 4522496 | tf_op jit(solution)/shard_map/exp | solution.py:64
  16.3 64.1 %gather_fusion = f32[16384,512]{1,0:T(8,128)} fusion(f32[256,512]{1,0:T(8,128)S(1)} %concatenate.10, s32[16384]{0:T(1024)S(1)} %fusion.10), kind=kCustom, calls=%fused_computation | custom fusion | bytes 67174400 | tf_op jit(solution)/shard_map/jit(_take)/gather | solution.py:71
  80.9 40.2 %all-gather.6.cloned.1.call-done = bf16[512,8192]{1,0:T(8,128)(2,1)} async-done(((bf16[512,512]{1,0:T(8,128)(2,1)}), bf16[512,8192]{1,0:T(8,128)(2,1)}) %all-gather.6.cloned.1.call-update) | async-done | bytes 8388624 | tf_op jit(solution)/shard_map/all_gather | solution.py:59
  121.1 6.9 %fusion.8 = (f32[128,512]{1,0:T(8,128)S(1)}, f32[128,512]{1,0:T(8,128)S(1)}) fusion(f32[3,128,512]{2,1,0:T(8,128)S(1)} %fusion.3, bf16[128,8192]{1,0:T(8,128)(2,1)} %all-gather.8.cloned.1.call-done, bf16[512,8192]{1,0:T(8,128)(2,1)} %all-gather.6.cloned.1.call-done), kind=kOutput, calls=%fused_computation.40 | convolution fusion | flops 1073807360 | bytes 11272192 | tf_op jit(solution)/shard_map/dot_general | solution.py:111
  128.2 3.1 %multiply_reduce_fusion.3 = (f32[512,16]{0,1:T(8,128)S(1)}, f32[512,16]{0,1:T(8,128)S(1)}) fusion(f32[128,16,512]{2,1,0:T(8,128)} %get-tuple-element.199, f32[512,128]{0,1:T(8,128)S(1)} %bitcast.129, f32[512,128]{0,1:T(8,128)S(1)} %multiply_bitcast_fusion.1), kind=kLoop, calls=%fused_computation.9 | loop fusion | flops 4177920 | bytes 4784128 | tf_op jit(solution)/shard_map/jnc,bjc->bnc/dot_general | solution.py:82
  131.3 17.1 %all-gather = bf16[256,512]{1,0:T(8,128)(2,1)S(1)} all-gather(bf16[16,512]{1,0:T(8,128)(2,1)S(1)} %get-tuple-element.205), channel_id=2, replica_groups=mesh['seq'=16,'ch'=16] {'seq'}, dimensions={0}, use_global_device_ids=true | all-gather | bytes 278528 | tf_op jit(solution)/shard_map/all_gather | solution.py:19
  148.5 16.2 %all-gather.2 = bf16[256,512]{1,0:T(8,128)(2,1)S(1)} all-gather(bf16[16,512]{1,0:T(8,128)(2,1)S(1)} %get-tuple-element.206), channel_id=4, replica_groups=mesh['seq'=16,'ch'=16] {'seq'}, dimensions={0}, use_global_device_ids=true | all-gather | bytes 278528 | tf_op jit(solution)/shard_map/all_gather | solution.py:19
  164.7 0.6 while.17
  165.3 15.6 %all-gather.1 = bf16[256,512]{1,0:T(8,128)(2,1)S(1)} all-gather(bf16[16,512]{1,0:T(8,128)(2,1)S(1)} %get-tuple-element.204), channel_id=3, replica_groups=mesh['seq'=16,'ch'=16] {'seq'}, dimensions={0}, use_global_device_ids=true | all-gather | bytes 278528 | tf_op jit(solution)/shard_map/all_gather | solution.py:19
  180.8 0.2 while.16
  181.1 18.0 %multiply_reduce_fusion = (f32[512,128]{0,1:T(8,128)S(1)}, f32[512,128]{0,1:T(8,128)S(1)}) fusion(f32[128,128,512]{2,1,0:T(8,128)} %bitcast.128, f32[512,128]{0,1:T(8,128)S(1)} %bitcast.130, pred[128,128]{1,0:T(8,128)(4,1)S(1)} %fusion.13, f32[512,128]{0,1:T(8,128)S(1)} %multiply_bitcast_fusion.1), kind=kLoop, calls=%fused_computation.5 | loop fusion | flops 41811968 | bytes 34619392 | tf_op jit(solution)/shard_map/ijc,bjc->bic/dot_general | solution.py:81
  199.1 2.5 multiply_reduce_fusion.2
  202.1 6.0 %convolution_convert_fusion = bf16[128,8192]{1,0:T(8,128)(2,1)} fusion(bf16[512,8192]{1,0:T(8,128)(2,1)} %all-gather.6.cloned.1.call-done, f32[128,512]{1,0:T(8,128)S(1)} %get-tuple-element.195, f32[3,128,512]{2,1,0:T(8,128)S(1)} %fusion.3), kind=kOutput, calls=%fused_computation.7 | convolution fusion | flops 1074921472 | bytes 11010048 | tf_op jit(solution)/shard_map/dot_general | solution.py:107
  208.1 3.4 %collective-permute-start.1 = (f32[3,2,512]{2,1,0:T(2,128)S(1)}, f32[3,2,512]{2,1,0:T(2,128)S(1)}, u32[]{:S(2)}, u32[]{:S(2)}) collective-permute-start(f32[3,2,512]{2,1,0:T(2,128)S(1)} %slice.75), channel_id=1, source_target_pairs={{16,0},{32,16},{48,32},{64,48},{80,64},{96,80},{112,96},{128,112},... | collective-permute-start | bytes 36872 | tf_op jit(solution)/shard_map/ppermute | solution.py:11
  211.5 1.4 collective-permute-done.1
  213.0 0.3 fusion.1
  213.2 0.8 slice_bitcast_fusion.1
  214.0 74.4 %reduce-scatter.2.cloned.1.call-done = bf16[128,512]{1,0:T(8,128)(2,1)} async-done(((bf16[128,8192]{1,0:T(8,128)(2,1)}), bf16[128,512]{1,0:T(8,128)(2,1)}) %reduce-scatter.2.cloned.1.call-update) | async-done | bytes 131088 | tf_op jit(solution)/shard_map/reduce_scatter | solution.py:108
  (50 shorter events, 1.7 us)
Async XLA Ops:
  7.2 73.7 %all-gather.8.cloned.1.call-start = ((), (), s32[]{:S(2)}) async-start(), calls=%async_computation.3 | async-start | bytes 2228224 | tf_op jit(solution)/shard_map/all_gather | solution.py:112
  7.9 113.2 %all-gather.6.cloned.1.call-start = ((), (), s32[]{:S(2)}) async-start(), calls=%async_computation.1 | async-start | bytes 8912896 | tf_op jit(solution)/shard_map/all_gather | solution.py:59
  8.6 279.7 %reduce-scatter.2.cloned.1.call-start = ((), (), s32[]{:S(2)}) async-start(), calls=%async_computation.2 | async-start | bytes 2228224 | tf_op jit(solution)/shard_map/reduce_scatter | solution.py:108
  9.4 71.0 %collective-permute-start = (bf16[3,2,512]{2,1,0:T(2,128)(2,1)S(1)}, bf16[3,2,512]{2,1,0:T(2,128)(2,1)S(1)}, u32[]{:S(2)}, u32[]{:S(2)}) collective-permute-start(bf16[3,2,512]{2,1,0:T(2,128)(2,1)S(1)} %pad_maximum_fusion.2), channel_id=1, source_target_pairs={{0,16},{16,32},{32,48},{48,64},{64,80},{80,96},{96,112},{112,128},... | collective-permute-start | bytes 18440 | tf_op jit(solution)/shard_map/ppermute | solution.py:11
  16.3 64.2 %copy-start = (bf16[128,512]{1,0:T(8,128)(2,1)S(1)}, bf16[128,512]{1,0:T(8,128)(2,1)}, u32[]{:S(2)}) copy-start(bf16[128,512]{1,0:T(8,128)(2,1)} %param.15) | copy-start | bytes 393220
  16.3 64.2 %copy-start.1 = (bf16[128,512]{1,0:T(8,128)(2,1)S(1)}, bf16[128,512]{1,0:T(8,128)(2,1)}, u32[]{:S(2)}) copy-start(bf16[128,512]{1,0:T(8,128)(2,1)} %param.14) | copy-start | bytes 393220
  16.3 64.2 %copy-start.2 = (bf16[128,512]{1,0:T(8,128)(2,1)S(1)}, bf16[128,512]{1,0:T(8,128)(2,1)}, u32[]{:S(2)}) copy-start(bf16[128,512]{1,0:T(8,128)(2,1)} %param.13) | copy-start | bytes 393220
  128.1 3.2 %copy-start.3 = (f32[16,512]{1,0:T(8,128)S(1)}, f32[16,512]{1,0:T(8,128)}, u32[]{:S(2)}) copy-start(f32[16,512]{1,0:T(8,128)} %param.17) | copy-start | bytes 98308
  181.1 20.7 %copy-start.4 = (f32[512]{0:T(512)S(1)}, f32[512]{0:T(512)}, u32[]{:S(2)}) copy-start(f32[512]{0:T(512)} %param.19) | copy-start | bytes 6148
  208.1 4.7 %collective-permute-start.1 = (f32[3,2,512]{2,1,0:T(2,128)S(1)}, f32[3,2,512]{2,1,0:T(2,128)S(1)}, u32[]{:S(2)}, u32[]{:S(2)}) collective-permute-start(f32[3,2,512]{2,1,0:T(2,128)S(1)} %slice.75), channel_id=1, source_target_pairs={{16,0},{32,16},{48,32},{64,48},{80,64},{96,80},{112,96},{128,112},... | collective-permute-start | bytes 36872 | tf_op jit(solution)/shard_map/ppermute | solution.py:11
Sparse Core Ops, SparseCore 0:
  10.4 55.2 all-gather.7
  67.6 53.5 all-gather.5
  208.2 80.1 reduce-scatter.1
where the time goes:
time: 295 us
  waiting for transfers between devices  117 us (40%)
  local copies, waits for them, and re-layouts  66 us (22%)
  blocking collectives  48.9 us (17%)
  other arithmetic  29.7 us (10%)
  between operations  14 us (5%)
  matrix products  12.9 us (4%)
  starting transfers between devices  5.38 us (2%)
    reduce_scatter x1, waiting for transfers between devices, per_device(): lax.psum_scatter(partial_value.astype(jnp.bfloat16), 'ch', scatter_dimens...  74.4 us
    gather x1, local copies, waits for them, and re-layouts, per_device(): toeplitz = jnp.take(filter_padded, lag_index, axis=0)  64.1 us
    all_gather x3, blocking collectives, entering(): lax.all_gather(a.astype(kind), axis)  48.9 us
    all_gather x1, waiting for transfers between devices, per_device(): columns = lax.all_gather(out_weight, 'seq', axis=1, tiled=True)  40.2 us
    dot_general x1, other arithmetic, local_pass(): intra = jnp.einsum('ijc,bjc->bic', toeplitz, blocks, precision=highest)  18 us
    dot_general x1, matrix products, per_device(): lax.dot_general(lax.all_gather(grad_out, 'ch', axis=1, tiled=True), colum...  6.94 us
    dot_general x1, matrix products, per_device(): partial_value = jnp.dot(mixer, columns, preferred_element_type=jnp.float32)  5.99 us
  transfers between devices with their start and end apart: 5, of which 3 were waited for; matrix products, arithmetic and copies ran while one was open for 24% of the time, Pallas kernels for 0%

commit v1 on v0

--- a/solution.py
+++ b/solution.py
@@ -56,7 +56,11 @@
     k_short = featured[1]
     v_short = featured[2]
     gated = k_short * v_short
-    columns = lax.all_gather(out_weight, "seq", axis=1, tiled=True)
+    form_lane = lambda mine_x, comm_axis, along_dim: jnp.concatenate(
+        jax.lax.all_to_all(jnp.stack(jax.lax.axis_size(comm_axis) * [mine_x]), comm_axis, 0, 0),
+        axis=along_dim,
+    )
+    columns = form_lane(out_weight, "seq", 1)
     block_len = math.gcd(tok_rows, 128)
     block_count = tok_rows // block_len
     mode_scale = residue * jnp.sqrt(-jnp.expm1(-2.0 * decay_rate))

time: 295 us -> 378 us (1.28)
  waiting for transfers between devices: 117 us -> 188 us
  starting transfers between devices: 5.38 us -> 14.4 us
  local copies, waits for them, and re-layouts: 66 us -> 70.7 us
    ppermute x2, waiting for transfers between devices: 1.39 us -> 112 us  [from_behind(): return lax.ppermute(block, axis, route)]
    all_gather x1 -> x0, waiting for transfers between devices: 40.2 us -> none  [per_device(): columns = lax.all_gather(out_weight, 'seq', axis=1, tiled=True)]
    all_to_all x0 -> x1, starting transfers between devices: none -> 8.73 us  [per_device(): jax.lax.all_to_all(jnp.stack(jax.lax.axis_size(comm_axis) * [mine_x]), co...]
    another operation x0 -> x1, local copies, waits for them, and re-layouts: none -> 4.01 us  [per_device(): jnp.stack(jax.lax.axis_size(comm_axis) * [mine_x])]
  transfers between devices with their start and end apart: 5 -> 5, of which waited for: 3 -> 4; matrix products, arithmetic and copies ran while one was open for 24% -> 18% of each run, Pallas kernels for 0% -> 0%
where the time goes in v1:
time: 378 us; the launch traced here: 377 us
  waiting for transfers between devices  188 us (50%)
  local copies, waits for them, and re-layouts  70.7 us (19%)
  blocking collectives  48.6 us (13%)
  other arithmetic  28.3 us (7%)
  starting transfers between devices  14.4 us (4%)
  between operations  14.4 us (4%)
  matrix products  12.8 us (3%)
    ppermute x2, waiting for transfers between devices, from_behind(): return lax.ppermute(block, axis, route)  112 us
    reduce_scatter x1, waiting for transfers between devices, per_device(): lax.psum_scatter(partial_value.astype(jnp.bfloat16), 'ch', scatter_dimens...  74.2 us
    gather x1, local copies, waits for them, and re-layouts, per_device(): toeplitz = jnp.take(filter_padded, lag_index, axis=0)  64.3 us
    all_gather x3, blocking collectives, entering(): lax.all_gather(a.astype(kind), axis)  48.6 us
    dot_general x1, other arithmetic, local_pass(): intra = jnp.einsum('ijc,bjc->bic', toeplitz, blocks, precision=highest)  18 us
    all_to_all x1, starting transfers between devices, per_device(): jax.lax.all_to_all(jnp.stack(jax.lax.axis_size(comm_axis) * [mine_x]), co...  8.73 us
  transfers between devices with their start and end apart: 5, of which 4 were waited for; matrix products, arithmetic and copies ran while one was open for 18% of the time, Pallas kernels for 0%

profile of v1, /device:TPU:32, one launch (start us, length us, event | category | flops | bytes accessed | tf_op | source)
XLA Modules:
  0.0 377.2 jit_solution(14537823993215702368)
XLA Ops:
  7.2 1.3 copy.14
  8.4 4.0 %stack.22 = bf16[16,512,512]{1,2,0:T(8,128)(2,1)} broadcast(bf16[512,512]{0,1:T(8,128)(2,1)S(1)} %copy.14), dimensions={1,2} | broadcast | bytes 8912896 | tf_op jit(solution)/shard_map/stack | solution.py:60
  12.5 8.7 %all-to-all-start = ((bf16[16,512,512]{1,2,0:T(8,128)(2,1)}), bf16[16,512,512]{1,2,0:T(8,128)(2,1)}, u32[]{:S(2)}, u32[]{:S(2)}) async-start(bf16[16,512,512]{1,2,0:T(8,128)(2,1)} %stack.22), calls=%async_computation | async-start | bytes 16777216 | tf_op jit(solution)/shard_map/all_to_all | solution.py:60
  21.2 0.7 all-gather.5.cloned.1.call-update
  22.0 2.1 collective-permute-start
  24.2 3.2 multiply_exponential_fusion
  27.7 64.3 %gather_fusion = f32[16384,512]{1,0:T(8,128)} fusion(f32[256,512]{1,0:T(8,128)S(1)} %concatenate.10, s32[16384]{0:T(1024)S(1)} %fusion.18), kind=kCustom, calls=%fused_computation | custom fusion | bytes 67174400 | tf_op jit(solution)/shard_map/jit(_take)/gather | solution.py:75
  91.9 110.9 %collective-permute-done = bf16[3,2,512]{2,1,0:T(2,128)(2,1)S(1)} collective-permute-done((bf16[3,2,512]{2,1,0:T(2,128)(2,1)S(1)}, bf16[3,2,512]{2,1,0:T(2,128)(2,1)S(1)}, u32[]{:S(2)}, u32[]{:S(2)}) %collective-permute-start) | collective-permute-done | bytes 6176 | tf_op jit(solution)/shard_map/ppermute | solution.py:11
  203.3 0.4 all-to-all-done
  203.6 5.3 %bitcast_multiply_fusion = (f32[128,512]{1,0:T(8,128)S(1)}, f32[128,512]{1,0:T(8,128)S(1)}) fusion(f32[3,128,512]{2,1,0:T(8,128)S(1)} %fusion.3, bf16[128,8192]{1,0:T(8,128)(2,1)} %all-gather.5.cloned.1.call-done, bf16[512,8192]{0,1:T(8,128)(2,1)} %bitcast.36), kind=kOutput, calls=%fused_computation.30 | convolution fusion | flops 1073807360 | bytes 11272192 | tf_op jit(solution)/shard_map/dot_general | solution.py:115
  209.0 3.1 multiply_reduce_fusion.3
  212.1 16.8 %all-gather = bf16[256,512]{1,0:T(8,128)(2,1)S(1)} all-gather(bf16[16,512]{1,0:T(8,128)(2,1)S(1)} %get-tuple-element.202), channel_id=2, replica_groups=mesh['seq'=16,'ch'=16] {'seq'}, dimensions={0}, use_global_device_ids=true | all-gather | bytes 278528 | tf_op jit(solution)/shard_map/all_gather | solution.py:19
  229.0 16.4 %all-gather.2 = bf16[256,512]{1,0:T(8,128)(2,1)S(1)} all-gather(bf16[16,512]{1,0:T(8,128)(2,1)S(1)} %get-tuple-element.203), channel_id=4, replica_groups=mesh['seq'=16,'ch'=16] {'seq'}, dimensions={0}, use_global_device_ids=true | all-gather | bytes 278528 | tf_op jit(solution)/shard_map/all_gather | solution.py:19
  245.4 0.6 while.17
  245.9 15.4 %all-gather.1 = bf16[256,512]{1,0:T(8,128)(2,1)S(1)} all-gather(bf16[16,512]{1,0:T(8,128)(2,1)S(1)} %get-tuple-element.201), channel_id=3, replica_groups=mesh['seq'=16,'ch'=16] {'seq'}, dimensions={0}, use_global_device_ids=true | all-gather | bytes 278528 | tf_op jit(solution)/shard_map/all_gather | solution.py:19
  261.4 0.2 while.16
  261.6 18.0 %multiply_reduce_fusion = (f32[512,128]{0,1:T(8,128)S(1)}, f32[512,128]{0,1:T(8,128)S(1)}) fusion(f32[128,128,512]{2,1,0:T(8,128)} %bitcast.138, f32[512,128]{0,1:T(8,128)S(1)} %bitcast.140, pred[128,128]{1,0:T(8,128)(4,1)S(1)} %fusion.21, f32[512,128]{0,1:T(8,128)S(1)} %fusion.16), kind=kLoop, calls=%fused_computation.5 | loop fusion | flops 41811968 | bytes 34619392 | tf_op jit(solution)/shard_map/ijc,bjc->bic/dot_general | solution.py:85
  279.6 2.5 multiply_reduce_fusion.2
  282.2 7.5 %convolution_convert_fusion = bf16[128,8192]{1,0:T(8,128)(2,1)} fusion(bf16[512,8192]{0,1:T(8,128)(2,1)} %bitcast.36, f32[3,128,512]{2,1,0:T(8,128)S(1)} %fusion.3, f32[512]{0:T(512)S(1)} %copy-done.4, f32[512,128]{0,1:T(8,128)S(1)} %get-tuple-element.165, f32[512,128]{0,1:T(8,128)S(1)} %get-tuple-element.169), kind=kOutput, calls=%fused_computation.7 | convolution fusion | flops 1075183616 | bytes 11798528 | tf_op jit(solution)/shard_map/dot_general | solution.py:111
  290.2 3.5 collective-permute-start.1
  293.7 1.4 collective-permute-done.1
  295.1 0.3 fusion.1
  295.4 0.8 slice_bitcast_fusion
  296.2 74.2 %reduce-scatter.2.cloned.1.call-done = bf16[128,512]{1,0:T(8,128)(2,1)} async-done(((bf16[128,8192]{1,0:T(8,128)(2,1)}), bf16[128,512]{1,0:T(8,128)(2,1)}) %reduce-scatter.2.cloned.1.call-update) | async-done | bytes 131088 | tf_op jit(solution)/shard_map/reduce_scatter | solution.py:112
  (55 shorter events, 1.7 us)
Async XLA Ops:
  12.4 9.5 %copy-start = (bf16[128,512]{1,0:T(8,128)(2,1)S(1)}, bf16[128,512]{1,0:T(8,128)(2,1)}, u32[]{:S(2)}) copy-start(bf16[128,512]{1,0:T(8,128)(2,1)} %param.15) | copy-start | bytes 393220
  12.4 9.6 %copy-start.1 = (bf16[128,512]{1,0:T(8,128)(2,1)S(1)}, bf16[128,512]{1,0:T(8,128)(2,1)}, u32[]{:S(2)}) copy-start(bf16[128,512]{1,0:T(8,128)(2,1)} %param.14) | copy-start | bytes 393220
  12.4 9.6 %copy-start.2 = (bf16[128,512]{1,0:T(8,128)(2,1)S(1)}, bf16[128,512]{1,0:T(8,128)(2,1)}, u32[]{:S(2)}) copy-start(bf16[128,512]{1,0:T(8,128)(2,1)} %param.13) | copy-start | bytes 393220
  12.4 11.7 %copy-start.6 = (f32[3,3,512]{2,1,0:T(4,128)S(1)}, f32[3,3,512]{2,1,0:T(4,128)}, u32[]{:S(2)}) copy-start(f32[3,3,512]{2,1,0:T(4,128)} %param.16) | copy-start | bytes 55300
  12.4 11.7 %copy-start.3 = (f32[16,512]{1,0:T(8,128)S(1)}, f32[16,512]{1,0:T(8,128)}, u32[]{:S(2)}) copy-start(f32[16,512]{1,0:T(8,128)} %param.17) | copy-start | bytes 98308
  12.5 11.7 %copy-start.5 = (f32[16,512]{1,0:T(8,128)S(1)}, f32[16,512]{1,0:T(8,128)}, u32[]{:S(2)}) copy-start(f32[16,512]{1,0:T(8,128)} %param.18) | copy-start | bytes 98308
  12.5 191.1 %all-to-all-start = ((bf16[16,512,512]{1,2,0:T(8,128)(2,1)}), bf16[16,512,512]{1,2,0:T(8,128)(2,1)}, u32[]{:S(2)}, u32[]{:S(2)}) async-start(bf16[16,512,512]{1,2,0:T(8,128)(2,1)} %stack.22), calls=%async_computation | async-start | bytes 16777216 | tf_op jit(solution)/shard_map/all_to_all | solution.py:60
  21.2 182.0 %all-gather.5.cloned.1.call-start = ((), (), s32[]{:S(2)}) async-start(), calls=%async_computation.3 | async-start | bytes 2228224 | tf_op jit(solution)/shard_map/all_gather | solution.py:116
  21.9 348.4 %reduce-scatter.2.cloned.1.call-start = ((), (), s32[]{:S(2)}) async-start(), calls=%async_computation.2 | async-start | bytes 2228224 | tf_op jit(solution)/shard_map/reduce_scatter | solution.py:112
  22.0 180.8 %collective-permute-start = (bf16[3,2,512]{2,1,0:T(2,128)(2,1)S(1)}, bf16[3,2,512]{2,1,0:T(2,128)(2,1)S(1)}, u32[]{:S(2)}, u32[]{:S(2)}) collective-permute-start(bf16[3,2,512]{2,1,0:T(2,128)(2,1)S(1)} %pad_maximum_fusion.2), channel_id=1, source_target_pairs={{0,16},{16,32},{32,48},{48,64},{64,80},{80,96},{96,112},{112,128},... | collective-permute-start | bytes 18440 | tf_op jit(solution)/shard_map/ppermute | solution.py:11
  261.6 20.5 %copy-start.4 = (f32[512]{0:T(512)S(1)}, f32[512]{0:T(512)}, u32[]{:S(2)}) copy-start(f32[512]{0:T(512)} %param.19) | copy-start | bytes 6148
  290.2 4.9 %collective-permute-start.1 = (f32[3,2,512]{2,1,0:T(2,128)S(1)}, f32[3,2,512]{2,1,0:T(2,128)S(1)}, u32[]{:S(2)}, u32[]{:S(2)}) collective-permute-start(f32[3,2,512]{2,1,0:T(2,128)S(1)} %slice.75), channel_id=1, source_target_pairs={{16,0},{32,16},{48,32},{64,48},{80,64},{96,80},{112,96},{128,112},... | collective-permute-start | bytes 36872 | tf_op jit(solution)/shard_map/ppermute | solution.py:11
Sparse Core Ops, SparseCore 0:
  24.4 53.8 all-gather.4
  289.8 80.4 reduce-scatter.1
